TPU v7x, 512 devices: a whole 4x4x16 slice. The times are simulated.
512 devices in a mesh: row: 32 (over z_lo, y), col: 16 (over z_hi, x, core).
Axes of the slice: x: 4, y: 4, z: 16 (z_hi: 2, z_lo: 8; z = z_hi * 8 + z_lo), core: 2. Of those that a mesh axis runs over, the one named last changes fastest.
Arguments:
- prefill_hidden: bfloat16 [4, 2048, 2880], P(None, 'row', 'col'), may hold values from -6 to 6
- decode_hidden: bfloat16 [128, 2880], P('row', 'col'), may hold values from -6 to 6
- norm_gain: bfloat16 [2880], replicated, may hold values from 0.5 to 1.5
- query_weight: bfloat16 [2880, 4096], P('row', 'col'), may hold values from -0.11388673 to 0.11388673
- kv_weight: bfloat16 [2880, 2, 512], P('row'), may hold values from -0.11388673 to 0.11388673
- out_weight: bfloat16 [4096, 2880], P('col', 'row'), may hold values from -0.09375 to 0.09375
- sink_logits: bfloat16 [64], P('col'), may hold values from -4 to 4
- key_pool: bfloat16 [768, 64, 512], P('row'), may hold values from -6 to 6
- value_pool: bfloat16 [768, 64, 512], P('row'), may hold values from -6 to 6
- lengths: int32 [32, 4], P('row'), may hold values from 1 to 384, 960 in all within a row
- page_table: int32 [32, 24], P('row'), may hold values from 0 to 23, each once within a row
Outputs:
- prefill_out: bfloat16 [4, 2048, 2880], P(None, 'row', 'col')
- decode_out: bfloat16 [128, 2880], P('row', 'col')
Inputs may be any that keep to these rules, and one draw needn't show every extreme that they name: The 4 cached lengths of one index of row sum to 960, and some request has length 384. `page_table`: each line lists every local page of one index of row exactly once; request r % 4 of that index owns entries (r % 4) * 6 to (r % 4 + 1) * 6 - 1.
All inputs are finite; a program needn't handle non-finite values.
Results may differ from a plain program's by a relative error of at most 0.012.
Values may be sent and summed in bfloat16 or wider, within the bound.
A program may use at most 64 MiB of HBM per device.

v0:
```python
import math
import jax
import jax.numpy as jnp
from jax import lax
from jax.sharding import PartitionSpec as P

HQ = 64
KV = 8
HD = 64


def normed(token_rows, norm_gain):
    widened = token_rows.astype(jnp.float32)
    inverse = lax.rsqrt(jnp.mean(widened * widened, axis=-1, keepdims=True) + 1e-05)
    return (widened * inverse * norm_gain.astype(jnp.float32)).astype(jnp.bfloat16)


def body(
    prefill_hidden,
    decode_hidden,
    norm_gain,
    query_weight,
    kv_weight,
    out_weight,
    sink_logits,
    key_pool,
    value_pool,
    lengths,
    page_table,
):
    spans, span_rows, col_width = prefill_hidden.shape
    decode_rows = decode_hidden.shape[0]
    prefill_count = spans * span_rows
    token_rows = jnp.concatenate(
        [prefill_hidden.reshape(prefill_count, col_width), decode_hidden], axis=0
    )
    features = lax.all_gather(token_rows, "col", axis=1, tiled=True)
    hidden = normed(features, norm_gain)
    heads_dev = query_weight.shape[1] // HD
    group_size = HQ // KV
    kv_dev = max(1, heads_dev // group_size)
    per_kv = heads_dev // kv_dev
    col_index = lax.axis_index("col")
    row_index = lax.axis_index("row")
    kv_first = col_index * heads_dev // group_size
    kv_columns = lax.dynamic_slice_in_dim(kv_weight, kv_first * HD, kv_dev * HD, 2).reshape(
        kv_weight.shape[0], 2 * kv_dev * HD
    )
    query_full, kv_full = (
        lax.all_gather(query_weight, "row", axis=0, tiled=True),
        lax.all_gather(kv_columns, "row", axis=0, tiled=True),
    )
    query_sum = jnp.dot(hidden, query_full, preferred_element_type=jnp.float32)
    kv_sum = jnp.dot(hidden, kv_full, preferred_element_type=jnp.float32)
    queries = query_sum.astype(jnp.bfloat16)
    key_rows = kv_sum[:, : kv_dev * HD].astype(jnp.bfloat16)
    value_rows = kv_sum[:, kv_dev * HD :].astype(jnp.bfloat16)
    score_scale = 1.0 / math.sqrt(HD)
    sink_grid = sink_logits.astype(jnp.float32).reshape(kv_dev, per_kv)
    query_pre = queries[:prefill_count].reshape(spans, span_rows, kv_dev, per_kv, HD)
    key_pre = key_rows[:prefill_count].reshape(spans, span_rows, kv_dev * HD)
    value_pre = value_rows[:prefill_count].reshape(spans, span_rows, kv_dev * HD)
    positions = row_index * span_rows + jnp.arange(span_rows, dtype=jnp.int32)
    state_shape = (spans, kv_dev, per_kv, span_rows)
    pieces = (
        lax.all_gather(key_pre, "row", axis=1, tiled=True),
        lax.all_gather(value_pre, "row", axis=1, tiled=True),
    )
    running = jnp.broadcast_to(sink_grid[None, :, :, None], state_shape)
    denominator = jnp.ones(state_shape, jnp.float32)
    weighted = jnp.zeros(state_shape + (HD,), jnp.float32)
    piece_len = pieces[0].shape[1]
    key_piece = pieces[0].reshape(spans, piece_len, kv_dev, HD)
    value_piece = pieces[1].reshape(spans, piece_len, kv_dev, HD)
    scores = (
        jnp.einsum("nqkgd,npkd->nkgqp", query_pre, key_piece, preferred_element_type=jnp.float32)
        * score_scale
    )
    key_pos = jnp.arange(piece_len, dtype=jnp.int32)
    allowed = key_pos[None, :] <= positions[:, None]
    scores = jnp.where(allowed, scores, -jnp.inf)
    newest = jnp.maximum(running, jnp.max(scores, axis=-1))
    probs_soft = jnp.exp(scores - newest[..., None])
    factor = jnp.exp(running - newest)
    denominator = denominator * factor + jnp.sum(probs_soft, axis=-1)
    weighted = weighted * factor[..., None] + jnp.einsum(
        "nkgqp,npkd->nkgqd",
        probs_soft.astype(jnp.bfloat16),
        value_piece,
        preferred_element_type=jnp.float32,
    )
    running, denominator, weighted = (newest, denominator, weighted)
    prefill_att = (
        (weighted / denominator[..., None])
        .transpose(0, 3, 1, 2, 4)
        .reshape(prefill_count, heads_dev * HD)
        .astype(jnp.bfloat16)
    )
    query_dec = queries[prefill_count:].reshape(decode_rows, kv_dev, per_kv, HD)
    key_new = key_rows[prefill_count:].reshape(decode_rows, kv_dev, HD)
    value_new = value_rows[prefill_count:].reshape(decode_rows, kv_dev, HD)
    pool_pages, page_len, pool_width = key_pool.shape
    table = page_table.reshape(decode_rows, -1)
    max_pages = table.shape[1]
    key_mine = lax.dynamic_slice_in_dim(
        key_pool.reshape(pool_pages, page_len, KV, HD), kv_first, kv_dev, 2
    )
    value_mine = lax.dynamic_slice_in_dim(
        value_pool.reshape(pool_pages, page_len, KV, HD), kv_first, kv_dev, 2
    )
    key_cache = key_mine[table].reshape(decode_rows, max_pages * page_len, kv_dev, HD)
    value_cache = value_mine[table].reshape(decode_rows, max_pages * page_len, kv_dev, HD)
    cache_scores = (
        jnp.einsum("skgd,stkd->skgt", query_dec, key_cache, preferred_element_type=jnp.float32)
        * score_scale
    )
    live = (
        jnp.arange(max_pages * page_len, dtype=jnp.int32)[None, :]
        < lengths.reshape(decode_rows)[:, None]
    )
    cache_scores = jnp.where(live[:, None, None, :], cache_scores, -jnp.inf)
    self_scores = (
        jnp.einsum("skgd,skd->skg", query_dec, key_new, preferred_element_type=jnp.float32)
        * score_scale
    )
    highest = jnp.maximum(jnp.maximum(jnp.max(cache_scores, axis=-1), self_scores), sink_grid[None])
    cache_probs = jnp.exp(cache_scores - highest[..., None])
    self_probs = jnp.exp(self_scores - highest)
    denom_dec = jnp.sum(cache_probs, axis=-1) + self_probs + jnp.exp(sink_grid[None] - highest)
    decode_sum = jnp.einsum(
        "skgt,stkd->skgd",
        cache_probs.astype(jnp.bfloat16),
        value_cache,
        preferred_element_type=jnp.float32,
    )
    decode_sum = (
        decode_sum
        + self_probs.astype(jnp.bfloat16).astype(jnp.float32)[..., None]
        * value_new.astype(jnp.float32)[:, :, None, :]
    )
    decode_att = (
        (decode_sum / denom_dec[..., None])
        .reshape(decode_rows, heads_dev * HD)
        .astype(jnp.bfloat16)
    )
    attended = jnp.concatenate([prefill_att, decode_att], axis=0)
    partial_out = jnp.dot(
        attended,
        lax.all_gather(out_weight, "row", axis=1, tiled=True),
        preferred_element_type=jnp.float32,
    )
    summed = lax.psum_scatter(
        partial_out.astype(jnp.bfloat16), "col", scatter_dimension=1, tiled=True
    ).astype(jnp.float32)
    result = (token_rows.astype(jnp.float32) + summed).astype(jnp.bfloat16)
    return (result[:prefill_count].reshape(spans, span_rows, col_width), result[prefill_count:])


def solution(mesh):
    in_specs = (
        P(None, "row", "col"),
        P("row", "col"),
        P(),
        P("row", "col"),
        P("row", None, None),
        P("col", "row"),
        P("col"),
        P("row", None, None),
        P("row", None, None),
        P("row", None),
        P("row", None),
    )
    out_specs = (P(None, "row", "col"), P("row", "col"))
    return jax.shard_map(body, mesh=mesh, in_specs=in_specs, out_specs=out_specs, check_vma=False)
```

profile of v0, /device:TPU:1, one launch (start us, length us, event | category | flops | bytes accessed | tf_op | source)
XLA Modules:
  0.0 1276.0 jit_solution(622490899157801376)
XLA Ops:
  7.2 1.6 fusion.37
  10.8 126.2 %all-gather.1 = bf16[32,90,128]{2,1,0:T(8,128)(2,1)S(1)} all-gather(bf16[1,90,128]{2,1,0:T(8,128)(2,1)S(1)} %copy.43), channel_id=1, replica_groups=mesh['row'=32,'col'=16] {'row'}, dimensions={0}, use_global_device_ids=true | all-gather | bytes 760320 | tf_op jit(solution)/shard_map/all_gather | solution.py:51
  138.1 4.2 copy_convert_fusion
  142.3 4.4 reshape.272
  149.4 5.1 reshape.231
  154.5 5.2 reshape.234
  159.7 5.5 constant_dynamic-slice_fusion
  167.3 2.0 copy.71
  169.3 2.4 gather_fusion
  171.7 2.4 gather_fusion.1
  174.6 128.9 %all-gather.16.cloned.1.call-done = bf16[32,90,256]{2,1,0:T(8,128)(2,1)} async-done(((bf16[1,90,256]{2,1,0:T(8,128)(2,1)}), bf16[32,90,256]{2,1,0:T(8,128)(2,1)}) %all-gather.16.cloned.1.call-update) | async-done | bytes 1474576 | tf_op jit(solution)/shard_map/all_gather | solution.py:50
  303.5 3.4 reshape.268
  306.9 2.1 convolution_convert_fusion.1
  309.4 1.3 fusion.52
  312.2 214.0 %all-gather.18.cloned.1.call-done = bf16[32,90,256]{2,1,0:T(8,128)(2,1)} async-done(((bf16[1,90,256]{2,1,0:T(8,128)(2,1)}), bf16[32,90,256]{2,1,0:T(8,128)(2,1)}) %all-gather.18.cloned.1.call-update) | async-done | bytes 1474576 | tf_op jit(solution)/shard_map/all_gather | solution.py:149
  526.2 2.3 reshape.270
  528.6 221.9 %all-gather.10.cloned.1.call-done = bf16[4,2048,64]{2,1,0:T(8,128)(2,1)} async-done(((bf16[4,64,64]{2,1,0:T(8,128)(2,1)}), bf16[4,2048,64]{2,1,0:T(8,128)(2,1)}) %all-gather.10.cloned.1.call-update) | async-done | bytes 1048592 | tf_op jit(solution)/shard_map/all_gather | solution.py:66
  750.5 3.1 fusion.2
  753.7 2.2 fusion
  756.9 217.0 %all-gather.12.cloned.1.call-done = bf16[4,2048,64]{2,1,0:T(8,128)(2,1)} async-done(((bf16[4,64,64]{2,1,0:T(8,128)(2,1)}), bf16[4,2048,64]{2,1,0:T(8,128)(2,1)}) %all-gather.12.cloned.1.call-update) | async-done | bytes 1048592 | tf_op jit(solution)/shard_map/all_gather | solution.py:67
  973.9 6.2 fusion.28
  980.5 1.8 convolution_convert_fusion
  982.3 1.3 dynamic-slice
  984.2 282.6 %all-reduce.3.cloned.1.call-done = bf16[260,2880]{1,0:T(8,128)(2,1)} async-done(((bf16[260,2880]{1,0:T(8,128)(2,1)}), bf16[260,2880]{1,0:T(8,128)(2,1)}) %all-reduce.3.cloned.1.call-update) | async-done | bytes 1497616
  (69 shorter events, 14.1 us)
Async XLA Ops:
  7.2 3.3 copy-start
  7.2 130.9 %copy-start.5 = (bf16[2880]{0:T(1024)(128)(2,1)S(1)}, bf16[2880]{0:T(1024)(128)(2,1)}, u32[]{:S(2)}) copy-start(bf16[2880]{0:T(1024)(128)(2,1)} %param.13) | copy-start | bytes 17284
  7.2 130.9 %all-gather.14.cloned.1.call-start = ((), (), s32[]{:S(2)}) async-start(), calls=%async_computation.2 | async-start | bytes 2297856 | tf_op jit(solution)/shard_map/all_gather | solution.py:37
  8.9 294.6 %all-gather.16.cloned.1.call-start = ((), (), s32[]{:S(2)}) async-start(), calls=%async_computation.3 | async-start | bytes 1622016 | tf_op jit(solution)/shard_map/all_gather | solution.py:50
  9.6 516.6 %all-gather.18.cloned.1.call-start = ((), (), s32[]{:S(2)}) async-start(), calls=%async_computation.4 | async-start | bytes 1622016 | tf_op jit(solution)/shard_map/all_gather | solution.py:149
  10.4 740.1 %all-gather.10.cloned.1.call-start = ((), (), s32[]{:S(2)}) async-start(), calls=%async_computation | async-start | bytes 2162688 | tf_op jit(solution)/shard_map/all_gather | solution.py:66
  146.7 1.1 copy-start.2
  146.7 2.6 copy-start.7
  149.3 824.6 %all-gather.12.cloned.1.call-start = ((), (), s32[]{:S(2)}) async-start(), calls=%async_computation.1 | async-start | bytes 2162688 | tf_op jit(solution)/shard_map/all_gather | solution.py:67
  159.7 6.8 copy-start.8
  159.7 14.4 %copy-start.6 = (s32[1,4]{1,0:T(1,128)S(1)}, s32[1,4]{1,0:T(1,128)}, u32[]{:S(2)}) copy-start(s32[1,4]{1,0:T(1,128)} %param.20) | copy-start | bytes 52
  174.3 1092.5 %all-reduce.3.cloned.1.call-start = ((), (), s32[]{:S(2)}) async-start(), calls=%async_computation.5 | async-start | bytes 3108864
  753.6 3.2 copy-start.1
  980.5 286.4 %copy-start.3 = (bf16[4,64,180]{2,1,0:T(8,128)(2,1)S(1)}, bf16[4,64,180]{2,1,0:T(8,128)(2,1)}, u32[]{:S(2)}) copy-start(bf16[4,64,180]{2,1,0:T(8,128)(2,1)} %param.11) | copy-start | bytes 276484
  980.5 286.4 %copy-start.4 = (bf16[4,180]{1,0:T(4,128)(2,1)S(1)}, bf16[4,180]{1,0:T(4,128)(2,1)}, u32[]{:S(2)}) copy-start(bf16[4,180]{1,0:T(4,128)(2,1)} %param.12) | copy-start | bytes 4324
Sparse Core Ops, SparseCore 0:
  11.2 99.8 all-gather.13
  113.1 190.3 all-gather.15
  305.6 220.6 all-gather.17
  528.8 221.7 all-gather.9
  752.4 221.4 all-gather.11
  982.4 284.3 all-reduce.2
where the time goes:
time: 1280 us
  waiting for transfers between devices  1070 us (84%)
  blocking collectives  126 us (10%)
  local copies, waits for them, and re-layouts  41.3 us (3%)
  matrix products  16.5 us (1%)
  between operations  15 us (1%)
    unnamed x7, waiting for transfers between devices  284 us
    all_gather x1, waiting for transfers between devices, body(): lax.all_gather(key_pre, 'row', axis=1, tiled=True)  222 us
    all_gather x1, waiting for transfers between devices, body(): lax.all_gather(value_pre, 'row', axis=1, tiled=True)  217 us
    all_gather x1, waiting for transfers between devices, body(): lax.all_gather(out_weight, 'row', axis=1, tiled=True)  214 us
    all_gather x1, waiting for transfers between devices, body(): lax.all_gather(query_weight, 'row', axis=0, tiled=True)  129 us
    all_gather x1, blocking collectives, body(): lax.all_gather(kv_columns, 'row', axis=0, tiled=True)  126 us
  transfers between devices with their start and end apart: 6, of which 5 were waited for; matrix products, arithmetic and copies ran while one was open for 4% of the time, Pallas kernels for 0%

commit v1 on v0

--- a/solution.py
+++ b/solution.py
@@ -47,7 +47,9 @@
         kv_weight.shape[0], 2 * kv_dev * HD
     )
     query_full, kv_full = (
-        lax.all_gather(query_weight, "row", axis=0, tiled=True),
+        jnp.concatenate(
+            lax.all_to_all(jnp.stack([query_weight] * lax.axis_size("row")), "row", 0, 0), axis=0
+        ),
         lax.all_gather(kv_columns, "row", axis=0, tiled=True),
     )
     query_sum = jnp.dot(hidden, query_full, preferred_element_type=jnp.float32)

time: 1280 us -> 1080 us (0.84)
  waiting for transfers between devices: 1070 us -> 838 us
  blocking collectives: 126 us -> 143 us
  starting transfers between devices: 0.42 us -> 16.7 us
    all_gather x1 -> x0, waiting for transfers between devices: 129 us -> none  [body(): lax.all_gather(query_weight, 'row', axis=0, tiled=True)]
    all_gather x1, waiting for transfers between devices: 214 us -> 123 us  [body(): lax.all_gather(out_weight, 'row', axis=1, tiled=True)]
    all_gather x1, blocking collectives: 126 us -> 143 us  [body(): lax.all_gather(kv_columns, 'row', axis=0, tiled=True)]
    all_to_all x0 -> x1, starting transfers between devices: none -> 16.3 us  [body(): lax.all_to_all(jnp.stack([query_weight] * lax.axis_size('row')), 'row', 0...]
    unnamed x7 -> x6, waiting for transfers between devices: 284 us -> 283 us
  transfers between devices with their start and end apart: 6 -> 6, of which waited for: 5 -> 4; matrix products, arithmetic and copies ran while one was open for 4% -> 5% of each run, Pallas kernels for 0% -> 0%
where the time goes in v1:
time: 1080 us
  waiting for transfers between devices  838 us (78%)
  blocking collectives  143 us (13%)
  local copies, waits for them, and re-layouts  45.1 us (4%)
  starting transfers between devices  16.7 us (2%)
  between operations  14.7 us (1%)
  matrix products  14.6 us (1%)
    unnamed x6, waiting for transfers between devices  283 us
    all_gather x1, waiting for transfers between devices, body(): lax.all_gather(value_pre, 'row', axis=1, tiled=True)  217 us
    all_gather x1, waiting for transfers between devices, body(): lax.all_gather(key_pre, 'row', axis=1, tiled=True)  215 us
    all_gather x1, blocking collectives, body(): lax.all_gather(kv_columns, 'row', axis=0, tiled=True)  143 us
    all_gather x1, waiting for transfers between devices, body(): lax.all_gather(out_weight, 'row', axis=1, tiled=True)  123 us
  transfers between devices with their start and end apart: 6, of which 4 were waited for; matrix products, arithmetic and copies ran while one was open for 5% of the time, Pallas kernels for 0%

profile of v1, /device:TPU:1, one launch (start us, length us, event | category | flops | bytes accessed | tf_op | source)
XLA Modules:
  0.0 1082.2 jit_solution(12201793037360066054)
XLA Ops:
  7.2 1.6 fusion.37
  8.9 2.2 stack.2
  11.1 16.3 %all-to-all-start = ((bf16[32,90,256]{2,1,0:T(8,128)(2,1)}), bf16[32,90,256]{2,1,0:T(8,128)(2,1)}, u32[]{:S(2)}, u32[]{:S(2)}) async-start(bf16[32,90,256]{2,1,0:T(8,128)(2,1)} %stack.2), calls=%async_computation | async-start | bytes 3145728 | tf_op jit(solution)/shard_map/all_to_all | solution.py:51
  28.6 142.7 %all-gather.1 = bf16[32,90,128]{2,1,0:T(8,128)(2,1)S(1)} all-gather(bf16[1,90,128]{2,1,0:T(8,128)(2,1)S(1)} %copy.43), channel_id=1, replica_groups=mesh['row'=32,'col'=16] {'row'}, dimensions={0}, use_global_device_ids=true | all-gather | bytes 760320 | tf_op jit(solution)/shard_map/all_gather | solution.py:53
  172.4 4.2 copy_convert_fusion
  176.6 4.4 reshape.276
  183.7 5.2 reshape.237
  188.8 5.1 reshape.240
  194.0 5.5 constant_dynamic-slice_fusion
  201.6 1.9 copy.71
  203.6 2.4 gather_fusion
  205.9 2.3 gather_fusion.1
  208.8 122.6 %all-gather.14.cloned.1.call-done = bf16[32,90,256]{2,1,0:T(8,128)(2,1)} async-done(((bf16[1,90,256]{2,1,0:T(8,128)(2,1)}), bf16[32,90,256]{2,1,0:T(8,128)(2,1)}) %all-gather.14.cloned.1.call-update) | async-done | bytes 1474576 | tf_op jit(solution)/shard_map/all_gather | solution.py:151
  331.4 3.4 reshape.274
  334.8 3.4 reshape.232
  338.2 2.1 convolution_convert_fusion.1
  341.1 214.7 %all-gather.8.cloned.1.call-done = bf16[4,2048,64]{2,1,0:T(8,128)(2,1)} async-done(((bf16[4,64,64]{2,1,0:T(8,128)(2,1)}), bf16[4,2048,64]{2,1,0:T(8,128)(2,1)}) %all-gather.8.cloned.1.call-update) | async-done | bytes 1048592 | tf_op jit(solution)/shard_map/all_gather | solution.py:68
  555.8 3.1 fusion.2
  558.9 2.2 fusion
  562.2 217.0 %all-gather.10.cloned.1.call-done = bf16[4,2048,64]{2,1,0:T(8,128)(2,1)} async-done(((bf16[4,64,64]{2,1,0:T(8,128)(2,1)}), bf16[4,2048,64]{2,1,0:T(8,128)(2,1)}) %all-gather.10.cloned.1.call-update) | async-done | bytes 1048592 | tf_op jit(solution)/shard_map/all_gather | solution.py:69
  779.2 6.3 fusion.28
  787.1 1.8 convolution_convert_fusion
  788.9 1.3 dynamic-slice
  790.8 282.6 %all-reduce.3.cloned.1.call-done = bf16[260,2880]{1,0:T(8,128)(2,1)} async-done(((bf16[260,2880]{1,0:T(8,128)(2,1)}), bf16[260,2880]{1,0:T(8,128)(2,1)}) %all-reduce.3.cloned.1.call-update) | async-done | bytes 1497616
  (78 shorter events, 13.3 us)
Async XLA Ops:
  7.2 21.1 %copy-start = (bf16[90,2,512]{2,1,0:T(2,128)(2,1)S(1)}, bf16[90,2,512]{2,1,0:T(2,128)(2,1)}, u32[]{:S(2)}) copy-start(bf16[90,2,512]{2,1,0:T(2,128)(2,1)} %param.15) | copy-start | bytes 552964
  7.2 165.3 %all-gather.12.cloned.1.call-start = ((), (), s32[]{:S(2)}) async-start(), calls=%async_computation.3 | async-start | bytes 2297856 | tf_op jit(solution)/shard_map/all_gather | solution.py:37
  11.1 161.3 %copy-start.9 = (bf16[2880]{0:T(1024)(128)(2,1)S(1)}, bf16[2880]{0:T(1024)(128)(2,1)}, u32[]{:S(2)}) copy-start(bf16[2880]{0:T(1024)(128)(2,1)} %param.13) | copy-start | bytes 17284
  11.1 323.7 %all-to-all-start = ((bf16[32,90,256]{2,1,0:T(8,128)(2,1)}), bf16[32,90,256]{2,1,0:T(8,128)(2,1)}, u32[]{:S(2)}, u32[]{:S(2)}) async-start(bf16[32,90,256]{2,1,0:T(8,128)(2,1)} %stack.2), calls=%async_computation | async-start | bytes 3145728 | tf_op jit(solution)/shard_map/all_to_all | solution.py:51
  27.4 304.0 %all-gather.14.cloned.1.call-start = ((), (), s32[]{:S(2)}) async-start(), calls=%async_computation.4 | async-start | bytes 1622016 | tf_op jit(solution)/shard_map/all_gather | solution.py:151
  28.2 527.6 %all-gather.8.cloned.1.call-start = ((), (), s32[]{:S(2)}) async-start(), calls=%async_computation.1 | async-start | bytes 2162688 | tf_op jit(solution)/shard_map/all_gather | solution.py:68
  181.0 1.1 copy-start.3
  181.0 2.6 copy-start.11
  183.6 595.6 %all-gather.10.cloned.1.call-start = ((), (), s32[]{:S(2)}) async-start(), calls=%async_computation.2 | async-start | bytes 2162688 | tf_op jit(solution)/shard_map/all_gather | solution.py:69
  194.0 6.8 copy-start.12
  194.0 14.3 %copy-start.10 = (s32[1,4]{1,0:T(1,128)S(1)}, s32[1,4]{1,0:T(1,128)}, u32[]{:S(2)}) copy-start(s32[1,4]{1,0:T(1,128)} %param.20) | copy-start | bytes 52
  208.5 864.9 %all-reduce.3.cloned.1.call-start = ((), (), s32[]{:S(2)}) async-start(), calls=%async_computation.5 | async-start | bytes 3108864
  340.3 0.7 copy-start.5
  558.9 3.2 copy-start.1
  779.2 6.8 slice-start
  779.2 7.0 copy-start.4
  779.2 7.5 copy-start.7
  779.2 7.9 copy-start.2
  787.0 286.5 %copy-start.6 = (bf16[4,64,180]{2,1,0:T(8,128)(2,1)S(1)}, bf16[4,64,180]{2,1,0:T(8,128)(2,1)}, u32[]{:S(2)}) copy-start(bf16[4,64,180]{2,1,0:T(8,128)(2,1)} %param.11) | copy-start | bytes 276484
  787.0 286.4 %copy-start.8 = (bf16[4,180]{1,0:T(4,128)(2,1)S(1)}, bf16[4,180]{1,0:T(4,128)(2,1)}, u32[]{:S(2)}) copy-start(bf16[4,180]{1,0:T(4,128)(2,1)} %param.12) | copy-start | bytes 4324
Sparse Core Ops, SparseCore 0:
  11.2 103.4 all-gather.11
  116.8 214.5 all-gather.13
  334.1 221.6 all-gather.7
  557.7 221.4 all-gather.9
  789.0 284.3 all-reduce.2
